TPU v7x, 32 devices: a whole 2x2x4 slice. The times are simulated.
32 devices in a mesh: lat: 4 (over y, x), lon: 2 (over core), lev: 4 (over z).
Axes of the slice: x: 2, y: 2, z: 4, core: 2. Of those that a mesh axis runs over, the one named last changes fastest.
Arguments:
- winds: float32 [16, 72, 2, 256], P('lat', 'lev', None, 'lon'), may hold values from -0.45 to 0.45
- mixing: float32 [16, 72, 72], P(('lat', 'lev')), may hold values from -0.12 to 0.7, as said below
- kernels: float32 [2048, 72], P(('lat', 'lon', 'lev')), may hold values from 0.2 to 1.2
- residuals: float32 [2048, 16], P(('lat', 'lon', 'lev')), may hold values from -6 to 6
- columns: int32 [2048], P(('lat', 'lon', 'lev')), may hold values from 0 to 127
- owners: int32 [2048, 1], P(('lat', 'lon', 'lev')), may hold values from 0 to 7; in each aligned block of 64 rows (0 to 63, 64 to 127, ...) at most 16 rows name the same one
- live_counts: int32 [32], P(('lat', 'lon', 'lev')), may hold values from 32 to 64, as said below
Outputs:
- gradient: float32 [16, 72, 16, 256], P('lat', 'lev', None, 'lon')
Inputs may be any that keep to these rules, and one draw needn't show every extreme that they name: Diagonal entries of every mixing matrix lie between 0.38 and 0.7, off-diagonal entries between -0.12 and 0.12, in every draw. The first live_counts[b] slots of device b's retrievals are live; some device has all 64 live. Column index row by row over the owner's 1 row of 128 columns. `owners`: at most 16 slots of one device name the same owner.
All inputs are finite; a program needn't handle non-finite values.
Results may differ from a plain program's by a relative error of at most 0.00022.
Values sent between devices are 32-bit elements; how exact they have to be, the bound alone decides.
A program may use at most 64 MiB of HBM per device.

v0:
```python
import jax
import jax.numpy as jnp
from jax import lax
from jax.sharding import PartitionSpec as P

STEPS = 4


def with_halo(block, sides, width):
    for axis, dim in sides:
        count = lax.axis_size(axis)
        forward = [(i, i + 1) for i in range(count - 1)]
        forward.append((count - 1, 0))
        backward = [(target, source) for source, target in forward]
        low = lax.ppermute(
            lax.slice_in_dim(block, block.shape[dim] - width, None, axis=dim), axis, forward
        )
        high = lax.ppermute(lax.slice_in_dim(block, 0, width, axis=dim), axis, backward)
        block = jnp.concatenate([low, block, high], axis=dim)
    return block


def transport(padded, winds, at_first, at_last):
    centre = padded[1:-1, :, :, 1:-1]
    east_side = padded[1:-1, :, :, 2:]
    west_side = padded[1:-1, :, :, :-2]
    north_side = padded[2:, :, :, 1:-1]
    south_side = padded[:-2, :, :, 1:-1]
    north_side = jnp.concatenate([north_side[:-1], jnp.where(at_last, centre, north_side)], axis=0)
    south_side = jnp.concatenate([jnp.where(at_first, centre, south_side), south_side[1:]], axis=0)
    zonal_wind = winds[:, :, 0:1, :]
    merid_wind = winds[:, :, 1:2, :]
    return (
        centre
        + jnp.maximum(zonal_wind, 0.0) * (east_side - centre)
        + jnp.minimum(zonal_wind, 0.0) * (centre - west_side)
        + jnp.maximum(merid_wind, 0.0) * (north_side - centre)
        + jnp.minimum(merid_wind, 0.0) * (centre - south_side)
    )


def mix_back(mixing, adjoint):
    return jnp.einsum("rjk,rjtl->rktl", mixing, adjoint, precision=lax.Precision.HIGHEST)


def deposit(summed, kern_rows, resid_part, col_ids):
    contrib = (kern_rows[:, :, None] * resid_part[:, None, :]).reshape(kern_rows.shape[0], -1)
    return summed.at[col_ids].add(contrib)


def shards(winds, mixing, kernels, residuals, columns, owners, live_counts):
    levels = mixing.shape[1]
    tracers = residuals.shape[1]
    slab_rows = mixing.shape[0]
    tile_cols = winds.shape[3]
    row_count = kernels.shape[0]
    lat_size = lax.axis_size("lat")
    lev_size = lax.axis_size("lev")
    my_index = lax.axis_index("lon") * lev_size + lax.axis_index("lev")
    live_mask = (jnp.arange(row_count) < live_counts[0]).astype(jnp.float32)
    resid_rows = residuals * live_mask[:, None]
    owner_ids = owners[:, 0]
    running = jnp.zeros((slab_rows * tile_cols, levels * tracers), jnp.float32)
    kern_part = lax.all_gather(kernels, ("lon", "lev"), axis=0, tiled=True)
    resid_part = lax.all_gather(resid_rows, ("lon", "lev"), axis=0, tiled=True)
    col_part = lax.all_gather(columns, ("lon", "lev"), axis=0, tiled=True)
    owner_part = lax.all_gather(owner_ids, ("lon", "lev"), axis=0, tiled=True)
    keep_mask = (owner_part == my_index).astype(jnp.float32)
    running = deposit(running, kern_part, resid_part * keep_mask[:, None], col_part)
    adjoint = running.reshape(slab_rows, tile_cols, levels, tracers).transpose(0, 2, 3, 1)
    wind_cols = lax.all_to_all(winds, "lev", split_axis=0, concat_axis=1, tiled=True)
    lat_pos = lax.axis_index("lat")
    lev_pos = lax.axis_index("lev")
    at_first = (lat_pos == 0) & (lev_pos == 0)
    at_last = (lat_pos == lat_size - 1) & (lev_pos == lev_size - 1)
    for sweep_index in range(STEPS):
        mixed = mix_back(mixing, adjoint)
        padded = with_halo(mixed, ((("lat", "lev"), 0), ("lon", 3)), 1)
        adjoint = transport(padded, wind_cols, at_first, at_last)
    gradient = lax.all_to_all(adjoint, "lev", split_axis=1, concat_axis=0, tiled=True)
    return gradient


def solution(mesh):
    return jax.shard_map(
        shards,
        mesh=mesh,
        in_specs=(
            P("lat", "lev", None, "lon"),
            P(("lat", "lev"), None, None),
            P(("lat", "lon", "lev"), None),
            P(("lat", "lon", "lev"), None),
            P(("lat", "lon", "lev")),
            P(("lat", "lon", "lev"), None),
            P(("lat", "lon", "lev")),
        ),
        out_specs=P("lat", "lev", None, "lon"),
        check_vma=False,
    )
```

profile of v0, /device:TPU:0, one launch (start us, length us, event | category | flops | bytes accessed | tf_op | source)
XLA Modules:
  0.0 261.8 jit_solution(14220002208314231462)
XLA Ops:
  0.7 1.2 dynamic-slice
  2.6 0.9 dynamic-update-slice
  3.4 0.7 bitcast_dynamic-update-slice_fusion
  4.2 10.7 %all-reduce.2 = (s32[512]{0:T(512)S(1)}, s32[512]{0:T(512)S(1)}) all-reduce(s32[512]{0:T(512)S(1)} %dynamic-update-slice, s32[512]{0:T(512)S(1)} %bitcast_dynamic-update-slice_fusion), channel_id=1, replica_groups=mesh['lat'=4,'lon'=2,'lev'=4] {'lon','lev'}, use_global_device_ids=true, to_apply=%add | all-reduce | flops 1024 | bytes 8192
  14.9 0.7 multiply_bitcast_fusion
  15.6 23.9 %all-gather.1 = f32[8,64,16]{1,2,0:T(8,128)S(1)} all-gather(f32[1,64,16]{1,2,0:T(8,128)S(1)} %multiply_bitcast_fusion), channel_id=1, replica_groups=mesh['lat'=4,'lon'=2,'lev'=4] {'lon','lev'}, dimensions={0}, use_global_device_ids=true | all-gather | bytes 36864 | tf_op jit(solution)/shard_map/all_gather | solution.py:65
  39.6 25.4 %all_gather.13 = f32[512,72]{1,0:T(8,128)S(1)} all-gather(f32[64,72]{1,0:T(8,128)} %param.9), channel_id=1, replica_groups=mesh['lat'=4,'lon'=2,'lev'=4] {'lon','lev'}, dimensions={0}, use_global_device_ids=true | all-gather | bytes 165888 | tf_op jit(solution)/shard_map/all_gather | solution.py:64
  65.5 2.0 copy.39
  67.5 6.4 %scatter_custom_fusion = f32[128,1152]{1,0:T(8,128)S(1)} fusion(s32[512]{0:T(512)S(1)} %compare_select_fusion, f32[512,1152]{1,0:T(8,128)} %copy.39, f32[]{:T(128)} %constant.8.clone.1), kind=kCustom, calls=%fused_computation.104 | custom fusion | flops 589824 | bytes 590336 | tf_op jit(solution)/shard_map/scatter-add | solution.py:48
  74.2 0.8 convolution_bitcast_fusion.3
  75.1 3.5 %collective-permute-start.1 = (f32[1,72,16,128]{3,1,2,0:T(8,128)S(1)}, f32[1,72,16,128]{3,1,2,0:T(8,128)S(1)}, u32[]{:S(2)}, u32[]{:S(2)}) collective-permute-start(f32[1,72,16,128]{3,1,2,0:T(8,128)S(1)} %convolution_bitcast_fusion.3), channel_id=1, source_target_pairs={{1,0},{2,1},{3,2},{8,3},{9,8},{10,9},{11,10},{16,11},{17,16},{18,1... | collective-permute-start | bytes 1769480 | tf_op jit(solution)/shard_map/ppermute | solution.py:18
  78.6 4.1 %all-to-all-start = ((f32[4,18,2,128]{3,2,1,0:T(2,128)}), f32[4,18,2,128]{3,2,1,0:T(2,128)S(1)}, u32[]{:S(2)}, u32[]{:S(2)}) async-start(f32[4,18,2,128]{3,2,1,0:T(2,128)} %param.7), calls=%async_computation | async-start | bytes 147456 | tf_op jit(solution)/shard_map/all_to_all | solution.py:71
  82.7 22.6 %all-to-all-done = f32[4,18,2,128]{3,2,1,0:T(2,128)S(1)} async-done(((f32[4,18,2,128]{3,2,1,0:T(2,128)}), f32[4,18,2,128]{3,2,1,0:T(2,128)S(1)}, u32[]{:S(2)}, u32[]{:S(2)}) %all-to-all-start) | async-done | bytes 73760 | tf_op jit(solution)/shard_map/all_to_all | solution.py:71
  106.3 0.8 copy-done.2
  107.2 1.8 fusion.92
  109.0 2.0 copy.44
  112.2 0.8 collective-permute-done.2
  113.6 1.9 copy.47
  115.5 2.7 %convolution_bitcast_fusion.2 = f32[1,72,16,128]{3,1,2,0:T(8,128)S(1)} fusion(f32[1,72,16,128]{3,1,2,0:T(8,128)S(1)} %convolution_bitcast_fusion.3, f32[1,72,16,128]{3,1,2,0:T(8,128)} %copy-done.1, f32[1,72,16,128]{3,1,2,0:T(8,128)} %copy-done.2, f32[3,72,16,1]{3,1,2,0:T(8,128)} %copy.47, f32[3,72,16,1]{3,1,2,0:T(8,128)S(1)} %copy.45, ...), kind=kOutput, calls=%fused_computation.7 | convolution fusion | flops 130351104 | bytes 2555138 | tf_op jit(solution)/shard_map/rjk,rjtl->rktl/dot_general | solution.py:43
  118.2 4.1 %collective-permute-start.5 = (f32[1,72,16,128]{3,1,2,0:T(8,128)S(1)}, f32[1,72,16,128]{3,1,2,0:T(8,128)S(1)}, u32[]{:S(2)}, u32[]{:S(2)}) collective-permute-start(f32[1,72,16,128]{3,1,2,0:T(8,128)S(1)} %convolution_bitcast_fusion.2), channel_id=1, source_target_pairs={{1,0},{2,1},{3,2},{8,3},{9,8},{10,9},{11,10},{16,11},{17,16},{18,1... | collective-permute-start | bytes 1769480 | tf_op jit(solution)/shard_map/ppermute | solution.py:18
  122.3 13.7 %collective-permute-done.5 = f32[1,72,16,128]{3,1,2,0:T(8,128)S(1)} collective-permute-done((f32[1,72,16,128]{3,1,2,0:T(8,128)S(1)}, f32[1,72,16,128]{3,1,2,0:T(8,128)S(1)}, u32[]{:S(2)}, u32[]{:S(2)}) %collective-permute-start.5) | collective-permute-done | bytes 589856 | tf_op jit(solution)/shard_map/ppermute | solution.py:18
  136.0 13.2 %collective-permute-done.4 = f32[1,72,16,128]{3,1,2,0:T(8,128)S(1)} collective-permute-done((f32[1,72,16,128]{3,1,2,0:T(8,128)S(1)}, f32[1,72,16,128]{3,1,2,0:T(8,128)S(1)}, u32[]{:S(2)}, u32[]{:S(2)}) %collective-permute-start.4) | collective-permute-done | bytes 589856 | tf_op jit(solution)/shard_map/ppermute | solution.py:15
  149.2 0.8 copy-done.6
  150.2 1.8 fusion.91
  152.0 2.0 copy.50
  155.3 0.6 copy.51
  156.1 1.9 copy.53
  157.9 2.7 %convolution_bitcast_fusion.1 = f32[1,72,16,128]{3,1,2,0:T(8,128)S(1)} fusion(f32[1,72,16,128]{3,1,2,0:T(8,128)S(1)} %convolution_bitcast_fusion.2, f32[1,72,16,128]{3,1,2,0:T(8,128)} %copy-done.4, f32[1,72,16,128]{3,1,2,0:T(8,128)} %copy-done.6, f32[3,72,16,1]{3,1,2,0:T(8,128)} %copy.53, f32[3,72,16,1]{3,1,2,0:T(8,128)S(1)} %copy.51, ...), kind=kOutput, calls=%fused_computation.6 | convolution fusion | flops 130351104 | bytes 2555138 | tf_op jit(solution)/shard_map/rjk,rjtl->rktl/dot_general | solution.py:43
  160.6 1.8 collective-permute-start.9
  162.7 13.8 %collective-permute-done.9 = f32[1,72,16,128]{3,1,2,0:T(8,128)S(1)} collective-permute-done((f32[1,72,16,128]{3,1,2,0:T(8,128)S(1)}, f32[1,72,16,128]{3,1,2,0:T(8,128)S(1)}, u32[]{:S(2)}, u32[]{:S(2)}) %collective-permute-start.9) | collective-permute-done | bytes 589856 | tf_op jit(solution)/shard_map/ppermute | solution.py:18
  176.5 12.8 %collective-permute-done.8 = f32[1,72,16,128]{3,1,2,0:T(8,128)S(1)} collective-permute-done((f32[1,72,16,128]{3,1,2,0:T(8,128)S(1)}, f32[1,72,16,128]{3,1,2,0:T(8,128)S(1)}, u32[]{:S(2)}, u32[]{:S(2)}) %collective-permute-start.8) | collective-permute-done | bytes 589856 | tf_op jit(solution)/shard_map/ppermute | solution.py:15
  189.3 0.8 copy-done.7
  190.2 1.8 fusion.90
  192.1 2.0 copy.55
  195.3 0.6 copy.56
  196.1 1.9 copy.58
  197.9 2.7 %convolution_bitcast_fusion = f32[1,72,16,128]{3,1,2,0:T(8,128)S(1)} fusion(f32[1,72,16,128]{3,1,2,0:T(8,128)S(1)} %convolution_bitcast_fusion.1, f32[1,72,16,128]{3,1,2,0:T(8,128)} %copy-done.5, f32[1,72,16,128]{3,1,2,0:T(8,128)} %copy-done.7, f32[3,72,16,1]{3,1,2,0:T(8,128)} %copy.58, f32[3,72,16,1]{3,1,2,0:T(8,128)S(1)} %copy.56, ...), kind=kOutput, calls=%fused_computation.5 | convolution fusion | flops 130351104 | bytes 2555138 | tf_op jit(solution)/shard_map/rjk,rjtl->rktl/dot_general | solution.py:43
  200.6 2.7 %collective-permute-start.13 = (f32[1,72,16,128]{3,1,2,0:T(8,128)S(1)}, f32[1,72,16,128]{3,1,2,0:T(8,128)S(1)}, u32[]{:S(2)}, u32[]{:S(2)}) collective-permute-start(f32[1,72,16,128]{3,1,2,0:T(8,128)S(1)} %convolution_bitcast_fusion), channel_id=1, source_target_pairs={{1,0},{2,1},{3,2},{8,3},{9,8},{10,9},{11,10},{16,11},{17,16},{18,1... | collective-permute-start | bytes 1769480 | tf_op jit(solution)/shard_map/ppermute | solution.py:18
  203.4 13.7 %collective-permute-done.13 = f32[1,72,16,128]{3,1,2,0:T(8,128)S(1)} collective-permute-done((f32[1,72,16,128]{3,1,2,0:T(8,128)S(1)}, f32[1,72,16,128]{3,1,2,0:T(8,128)S(1)}, u32[]{:S(2)}, u32[]{:S(2)}) %collective-permute-start.13) | collective-permute-done | bytes 589856 | tf_op jit(solution)/shard_map/ppermute | solution.py:18
  217.1 14.2 %collective-permute-done.12 = f32[1,72,16,128]{3,1,2,0:T(8,128)S(1)} collective-permute-done((f32[1,72,16,128]{3,1,2,0:T(8,128)S(1)}, f32[1,72,16,128]{3,1,2,0:T(8,128)S(1)}, u32[]{:S(2)}, u32[]{:S(2)}) %collective-permute-start.12) | collective-permute-done | bytes 589856 | tf_op jit(solution)/shard_map/ppermute | solution.py:15
  231.3 0.8 copy-done.3
  232.3 1.8 fusion.89
  234.1 2.0 copy.60
  237.4 0.6 copy.61
  238.1 1.9 copy.63
  240.0 1.8 fusion.23
  241.9 19.1 %all_to_all.24 = f32[1,72,16,128]{3,2,0,1:T(8,128)S(1)} all-to-all(f32[1,72,16,128]{3,2,0,1:T(8,128)S(1)} %copy.64), channel_id=1, replica_groups=mesh['lat'=4,'lon'=2,'lev'=4] {'lev'}, dimensions={1} | all-to-all | bytes 1179648 | tf_op jit(solution)/shard_map/all_to_all | solution.py:80
  261.0 0.8 copy.83
  (56 shorter events, 8.6 us)
Async XLA Ops:
  0.0 74.2 %copy-start = (f32[1,72,72]{2,1,0:T(8,128)S(1)}, f32[1,72,72]{2,1,0:T(8,128)}, u32[]{:S(2)}) copy-start(f32[1,72,72]{2,1,0:T(8,128)} %param.8) | copy-start | bytes 62212
  75.1 30.3 %collective-permute-start.1 = (f32[1,72,16,128]{3,1,2,0:T(8,128)S(1)}, f32[1,72,16,128]{3,1,2,0:T(8,128)S(1)}, u32[]{:S(2)}, u32[]{:S(2)}) collective-permute-start(f32[1,72,16,128]{3,1,2,0:T(8,128)S(1)} %convolution_bitcast_fusion.3), channel_id=1, source_target_pairs={{1,0},{2,1},{3,2},{8,3},{9,8},{10,9},{11,10},{16,11},{17,16},{18,1... | collective-permute-start | bytes 1769480 | tf_op jit(solution)/shard_map/ppermute | solution.py:18
  78.6 27.1 %collective-permute-start = (f32[1,72,16,128]{3,1,2,0:T(8,128)S(1)}, f32[1,72,16,128]{3,1,2,0:T(8,128)S(1)}, u32[]{:S(2)}, u32[]{:S(2)}) collective-permute-start(f32[1,72,16,128]{3,1,2,0:T(8,128)S(1)} %convolution_bitcast_fusion.3), channel_id=1, source_target_pairs={{0,1},{1,2},{2,3},{3,8},{8,9},{9,10},{10,11},{11,16},{16,17},{17,1... | collective-permute-start | bytes 1769480 | tf_op jit(solution)/shard_map/ppermute | solution.py:15
  78.6 26.7 %all-to-all-start = ((f32[4,18,2,128]{3,2,1,0:T(2,128)}), f32[4,18,2,128]{3,2,1,0:T(2,128)S(1)}, u32[]{:S(2)}, u32[]{:S(2)}) async-start(f32[4,18,2,128]{3,2,1,0:T(2,128)} %param.7), calls=%async_computation | async-start | bytes 147456 | tf_op jit(solution)/shard_map/all_to_all | solution.py:71
  105.4 0.8 copy-start.1
  106.3 0.8 copy-start.2
  111.6 2.0 collective-permute-start.3
  111.7 1.3 collective-permute-start.2
  118.2 17.8 %collective-permute-start.5 = (f32[1,72,16,128]{3,1,2,0:T(8,128)S(1)}, f32[1,72,16,128]{3,1,2,0:T(8,128)S(1)}, u32[]{:S(2)}, u32[]{:S(2)}) collective-permute-start(f32[1,72,16,128]{3,1,2,0:T(8,128)S(1)} %convolution_bitcast_fusion.2), channel_id=1, source_target_pairs={{1,0},{2,1},{3,2},{8,3},{9,8},{10,9},{11,10},{16,11},{17,16},{18,1... | collective-permute-start | bytes 1769480 | tf_op jit(solution)/shard_map/ppermute | solution.py:18
  122.3 27.0 %collective-permute-start.4 = (f32[1,72,16,128]{3,1,2,0:T(8,128)S(1)}, f32[1,72,16,128]{3,1,2,0:T(8,128)S(1)}, u32[]{:S(2)}, u32[]{:S(2)}) collective-permute-start(f32[1,72,16,128]{3,1,2,0:T(8,128)S(1)} %convolution_bitcast_fusion.2), channel_id=1, source_target_pairs={{0,1},{1,2},{2,3},{3,8},{8,9},{9,10},{10,11},{11,16},{16,17},{17,1... | collective-permute-start | bytes 1769480 | tf_op jit(solution)/shard_map/ppermute | solution.py:15
  136.0 13.2 %copy-start.4 = (f32[1,72,16,128]{3,1,2,0:T(8,128)}, f32[1,72,16,128]{3,1,2,0:T(8,128)S(1)}, u32[]{:S(2)}) copy-start(f32[1,72,16,128]{3,1,2,0:T(8,128)S(1)} %collective-permute-done.5) | copy-start | bytes 1769476
  149.2 0.8 copy-start.6
  154.1 1.2 collective-permute-start.6
  154.7 1.4 collective-permute-start.7
  160.6 15.9 %collective-permute-start.9 = (f32[1,72,16,128]{3,1,2,0:T(8,128)S(1)}, f32[1,72,16,128]{3,1,2,0:T(8,128)S(1)}, u32[]{:S(2)}, u32[]{:S(2)}) collective-permute-start(f32[1,72,16,128]{3,1,2,0:T(8,128)S(1)} %convolution_bitcast_fusion.1), channel_id=1, source_target_pairs={{1,0},{2,1},{3,2},{8,3},{9,8},{10,9},{11,10},{16,11},{17,16},{18,1... | collective-permute-start | bytes 1769480 | tf_op jit(solution)/shard_map/ppermute | solution.py:18
  162.4 26.9 %collective-permute-start.8 = (f32[1,72,16,128]{3,1,2,0:T(8,128)S(1)}, f32[1,72,16,128]{3,1,2,0:T(8,128)S(1)}, u32[]{:S(2)}, u32[]{:S(2)}) collective-permute-start(f32[1,72,16,128]{3,1,2,0:T(8,128)S(1)} %convolution_bitcast_fusion.1), channel_id=1, source_target_pairs={{0,1},{1,2},{2,3},{3,8},{8,9},{9,10},{10,11},{11,16},{16,17},{17,1... | collective-permute-start | bytes 1769480 | tf_op jit(solution)/shard_map/ppermute | solution.py:15
  176.5 12.8 %copy-start.5 = (f32[1,72,16,128]{3,1,2,0:T(8,128)}, f32[1,72,16,128]{3,1,2,0:T(8,128)S(1)}, u32[]{:S(2)}) copy-start(f32[1,72,16,128]{3,1,2,0:T(8,128)S(1)} %collective-permute-done.9) | copy-start | bytes 1769476
  189.3 0.8 copy-start.7
  194.1 1.2 collective-permute-start.10
  194.7 1.4 collective-permute-start.11
  200.6 16.4 %collective-permute-start.13 = (f32[1,72,16,128]{3,1,2,0:T(8,128)S(1)}, f32[1,72,16,128]{3,1,2,0:T(8,128)S(1)}, u32[]{:S(2)}, u32[]{:S(2)}) collective-permute-start(f32[1,72,16,128]{3,1,2,0:T(8,128)S(1)} %convolution_bitcast_fusion), channel_id=1, source_target_pairs={{1,0},{2,1},{3,2},{8,3},{9,8},{10,9},{11,10},{16,11},{17,16},{18,1... | collective-permute-start | bytes 1769480 | tf_op jit(solution)/shard_map/ppermute | solution.py:18
  203.3 27.9 %collective-permute-start.12 = (f32[1,72,16,128]{3,1,2,0:T(8,128)S(1)}, f32[1,72,16,128]{3,1,2,0:T(8,128)S(1)}, u32[]{:S(2)}, u32[]{:S(2)}) collective-permute-start(f32[1,72,16,128]{3,1,2,0:T(8,128)S(1)} %convolution_bitcast_fusion), channel_id=1, source_target_pairs={{0,1},{1,2},{2,3},{3,8},{8,9},{9,10},{10,11},{11,16},{16,17},{17,1... | collective-permute-start | bytes 1769480 | tf_op jit(solution)/shard_map/ppermute | solution.py:15
  231.3 0.8 copy-start.3
  236.1 1.2 collective-permute-start.14
  236.8 1.4 collective-permute-start.15
where the time goes:
time: 262 us
  waiting for transfers between devices  106 us (40%)
  blocking collectives  79.2 us (30%)
  local copies, waits for them, and re-layouts  37.5 us (14%)
  starting transfers between devices  18.9 us (7%)
  other arithmetic  9.9 us (4%)
  matrix products  8.81 us (3%)
    ppermute x8, waiting for transfers between devices, with_halo(): lax.ppermute(lax.slice_in_dim(block, 0, width, axis=dim), axis, backward)  42.3 us
    ppermute x8, waiting for transfers between devices, with_halo(): lax.ppermute(lax.slice_in_dim(block, block.shape[dim] - width, None, axis...  41 us
    all_gather x1, blocking collectives, shards(): kern_part = lax.all_gather(kernels, ('lon', 'lev'), axis=0, tiled=True)  25.4 us
    all_gather x1, blocking collectives, shards(): resid_part = lax.all_gather(resid_rows, ('lon', 'lev'), axis=0, tiled=True)  23.9 us
    all_to_all x1, waiting for transfers between devices, shards(): lax.all_to_all(winds, 'lev', split_axis=0, concat_axis=1, tiled=True)  22.6 us
    all_to_all x1, blocking collectives, shards(): lax.all_to_all(adjoint, 'lev', split_axis=1, concat_axis=0, tiled=True)  19.1 us
    slice x8, local copies, waits for them, and re-layouts, with_halo(): lax.slice_in_dim(block, 0, width, axis=dim)  15.4 us
    ppermute x8, starting transfers between devices, with_halo(): lax.ppermute(lax.slice_in_dim(block, 0, width, axis=dim), axis, backward)  12.8 us
  transfers between devices with their start and end apart: 17, of which 15 were waited for; matrix products, arithmetic and copies ran while one was open for 2% of the time, Pallas kernels for 0%

commit v1 on v0

--- a/solution.py
+++ b/solution.py
@@ -1,6 +1,8 @@
 import jax
 import jax.numpy as jnp
 from jax import lax
+from jax.experimental import pallas as pl
+from jax.experimental.pallas import tpu as pltpu
 from jax.sharding import PartitionSpec as P
 
 STEPS = 4
@@ -81,9 +83,297 @@
     return gradient
 
 
+LEVELS = 72
+TRACERS = 16
+MESH = pl.DeviceIdType.MESH
+F32 = jnp.float32
+BF16 = jnp.bfloat16
+
+
+def window_kernel(
+    pm_ref, w_ref, out_ref, gp, gw, state, mixed, mix_stack, wind, halo, stage, vals, spots,
+    send_p, recv_p, send_w, recv_w, send_h, recv_h, send_o, recv_o,
+):
+    lat, o, z = lax.axis_index("lat"), lax.axis_index("lon"), lax.axis_index("lev")
+    y, x = lat // 2, lat % 2
+    me = (x * 2 + o) * 4 + z
+    other_x, other_o = (lat - x) + (1 - x), 1 - o
+    across = (1 - y) * 2 + x
+
+    def member(s):
+        return ((lat - x) + s // 8, (s // 4) % 2, s % 4)
+
+    def device_of(d):
+        return member((me + d) % 16)
+
+    barrier = pltpu.get_barrier_semaphore()
+    for d in range(1, 16):
+        pl.semaphore_signal(barrier, inc=1, device_id=device_of(d), device_id_type=MESH)
+    pl.semaphore_signal(barrier, inc=1, device_id=(across, o, z), device_id_type=MESH)
+    pl.semaphore_wait(barrier, 16)
+
+    def make(refs, at, src, send, recv, xx, oo, zz, k, device):
+        return pltpu.make_async_remote_copy(
+            src_ref=at(xx, oo, zz) if src is None else src,
+            dst_ref=at(xx, oo, zz),
+            send_sem=send.at[k],
+            recv_sem=recv.at[(xx * 2 + oo) * 4 + zz],
+            device_id=device,
+            device_id_type=MESH,
+        )
+
+    def at_p(xx, oo, zz):
+        return gp.at[(xx * 2 + oo) * 4 + zz]
+
+    def at_w(xx, oo, zz):
+        return gw.at[xx * 2 + oo, pl.ds(pl.multiple_of(zz * 144, 8), 144)]
+
+    sent = []
+
+    def first(at, src, send, recv):
+        for d in range(1, 4):
+            copy = make(None, at, src, send, recv, x, o, z, d - 1, (lat, o, (z + d) % 4))
+            copy.start()
+            sent.append(copy)
+
+    def second(at, src, send, recv):
+        for d in range(4):
+            zz = (z + d) % 4
+            if d:
+                make(None, at, None, send, recv, x, o, zz, 0, (lat, o, z)).wait_recv()
+            own = src if d == 0 else None
+            a = make(None, at, own, send, recv, x, o, zz, 3 + d, (other_x, o, z))
+            a.start()
+            b = make(None, at, own, send, recv, x, o, zz, 7 + d, (lat, other_o, z))
+            b.start()
+            sent.extend([a, b])
+
+    def third(at, send, recv):
+        for d in range(4):
+            zz = (z + d) % 4
+            make(None, at, None, send, recv, 1 - x, o, zz, 0, (lat, o, z)).wait_recv()
+            c = make(None, at, None, send, recv, 1 - x, o, zz, 11 + d, (lat, other_o, z))
+            c.start()
+            sent.append(c)
+
+    def rest(at, send, recv):
+        for xx in (x, 1 - x):
+            for d in range(4):
+                make(None, at, None, send, recv, xx, 1 - o, (z + d) % 4, 0, (lat, o, z)).wait_recv()
+
+    first(at_p, pm_ref, send_p, recv_p)
+    first(at_w, w_ref, send_w, recv_w)
+    gp[me] = pm_ref[...]
+    gw[x * 2 + o, pl.ds(pl.multiple_of(z * 144, 8), 144)] = w_ref[...]
+    second(at_p, pm_ref, send_p, recv_p)
+    third(at_p, send_p, recv_p)
+    second(at_w, w_ref, send_w, recv_w)
+    rest(at_p, send_p, recv_p)
+
+    def place(i):
+        return y * i + (1 - y) * (7 - i)
+
+    lane = lax.broadcasted_iota(jnp.int32, (512, 128), 1)
+    for xx in range(2):
+        rows = gp[xx * 8:xx * 8 + 8, 0:64, :].reshape(512, 128)
+        resid = jnp.sum(jnp.where(lane == LEVELS + me, rows, 0.0), axis=1, keepdims=True)
+        spot = jnp.sum(jnp.where(lane == LEVELS + TRACERS, rows, 0.0), axis=1, keepdims=True)
+        spots[xx] = jnp.broadcast_to(spot, (512, 128)).astype(jnp.int32)
+        terms = (rows * resid).T[:LEVELS]
+        high = terms.astype(BF16).astype(F32)
+        vals[xx] = jnp.concatenate([high, terms - high], axis=0).astype(BF16)
+
+    def prepare(i, carry):
+        n = place(i)
+        for half in range(2):
+            hits = spots[i // 4] == lane + ((i % 4) * 256 + half * 128)
+            ones = jnp.where(hits, 1.0, 0.0).astype(BF16)
+            both = jnp.dot(vals[i // 4], ones, preferred_element_type=F32)
+            state[n, :, half * 128:half * 128 + 128] = both[:LEVELS] + both[LEVELS:]
+        mat = gp[(i // 4) * 8 + i % 4, 64:136, 0:LEVELS]
+        high = mat.astype(BF16).astype(F32)
+        mix_stack[n] = jnp.concatenate([high, mat - high, high], axis=1).astype(BF16)
+        return carry
+
+    lax.fori_loop(0, 8, prepare, 0)
+    third(at_w, send_w, recv_w)
+
+    def mix(n, carry):
+        col = state[n]
+        high = col.astype(BF16).astype(F32)
+        stack = jnp.concatenate([high, high, col - high], axis=0).astype(BF16)
+        mixed[n] = jnp.dot(mix_stack[n], stack, preferred_element_type=F32)
+        return carry
+
+    def moved(n, before, after):
+        c = mixed[n]
+        u, v = wind[n, 0], wind[n, 1]
+        east = pltpu.roll(c, 255, axis=1)
+        west = pltpu.roll(c, 1, axis=1)
+        return (
+            c
+            + jnp.maximum(u, 0.0) * (east - c)
+            + jnp.minimum(u, 0.0) * (c - west)
+            + jnp.maximum(v, 0.0) * (before - c)
+            + jnp.minimum(v, 0.0) * (c - after)
+        )
+
+    def winds_in(i, carry):
+        n = place(i)
+        for half in range(2):
+            for comp in range(2):
+                part = gw[(i // 4) * 2 + half, pl.ds((i % 4) * 2 + comp, LEVELS, stride=8), :]
+                if comp == 1:
+                    part = part * (1 - 2 * y).astype(F32)
+                wind[n, comp, :, half * 128:half * 128 + 128] = part
+        return carry
+
+    def put(n, new):
+        i = place(n)
+        for half in range(2):
+            stage[i // 4, half, pl.ds(i % 4, LEVELS, stride=4), :] = new[:, half * 128:half * 128 + 128]
+
+    def halo_copy(step):
+        return pltpu.make_async_remote_copy(
+            src_ref=mixed.at[0],
+            dst_ref=halo.at[step],
+            send_sem=send_h.at[step],
+            recv_sem=recv_h.at[step],
+            device_id=(across, o, z),
+            device_id_type=MESH,
+        )
+
+    for step in range(STEPS):
+        last = step == STEPS - 1
+        mix(0, 0)
+        copy = halo_copy(step)
+        copy.start()
+        lax.fori_loop(1, 8, mix, 0)
+        if step == 0:
+            rest(at_w, send_w, recv_w)
+            lax.fori_loop(0, 8, winds_in, 0)
+
+        def carry_on(n, carry):
+            new = moved(n, mixed[n - 1], mixed[jnp.minimum(n + 1, 7)])
+            if last:
+                put(n, new)
+            else:
+                state[n] = new
+            return carry
+
+        def ship(far):
+            xx = y if far else 1 - y
+            copies = []
+            for half in range(2):
+                for d in range(4):
+                    zz = (z + d) % 4
+                    k = (0 if far else 8) + half * 4 + d
+                    copies.append(((xx, half, zz, d), pltpu.make_async_remote_copy(
+                        src_ref=stage.at[xx, half, pl.ds(pl.multiple_of(zz * 72, 8), 72)],
+                        dst_ref=out_ref.at[me],
+                        send_sem=send_o.at[k],
+                        recv_sem=recv_o.at[me],
+                        device_id=((lat - x) + xx, half, zz),
+                        device_id_type=MESH,
+                    )))
+            return copies
+
+        if not last:
+            lax.fori_loop(1, 8, carry_on, 0)
+            copy.wait()
+            state[0] = moved(0, halo[step], mixed[1])
+        else:
+            lax.fori_loop(4, 8, carry_on, 0)
+            far = ship(True)
+            near = ship(False)
+
+            def launch(copies):
+                for (xx, half, zz, d), one in copies:
+                    if d:
+                        one.start()
+                    else:
+                        mine = (xx == x) & (half == o)
+
+                        @pl.when(mine)
+                        def _():
+                            out_ref[me] = stage[xx, half, pl.ds(pl.multiple_of(zz * 72, 8), 72), :]
+
+                        @pl.when(jnp.logical_not(mine))
+                        def _():
+                            one.start()
+
+            launch(far)
+            lax.fori_loop(1, 4, carry_on, 0)
+            copy.wait()
+            put(0, moved(0, halo[step], mixed[1]))
+            launch(near)
+            for (xx, half, zz, d), one in far + near:
+                if d:
+                    one.wait_send()
+                else:
+
+                    @pl.when(jnp.logical_not((xx == x) & (half == o)))
+                    def _():
+                        one.wait_send()
+
+            for d in range(1, 16):
+                s = (me + d) % 16
+                pltpu.make_async_remote_copy(
+                    src_ref=out_ref.at[s],
+                    dst_ref=out_ref.at[s],
+                    send_sem=send_o.at[0],
+                    recv_sem=recv_o.at[s],
+                    device_id=(lat, o, z),
+                    device_id_type=MESH,
+                ).wait_recv()
+    for one in sent:
+        one.wait_send()
+
+
+def fast_shards(winds, mixing, kernels, residuals, columns, owners, live_counts):
+    row_count = kernels.shape[0]
+    live = (jnp.arange(row_count) < live_counts[0]).astype(F32)
+    own = owners[:, 0]
+    spot = (own % 4) * 256 + (own // 4) * 128 + columns % 128
+    rows = jnp.concatenate(
+        [kernels, residuals * live[:, None], spot.astype(F32)[:, None],
+         jnp.zeros((row_count, 128 - LEVELS - TRACERS - 1), F32)], axis=1)
+    matrix = jnp.pad(mixing[0].T, ((0, 0), (0, 128 - LEVELS)))
+    pm = jnp.concatenate([rows, matrix], axis=0)
+    wind_rows = winds.transpose(1, 0, 2, 3).reshape(144, 128)
+    dma = pltpu.SemaphoreType.DMA
+    whole = pl.BlockSpec(memory_space=pltpu.VMEM)
+    out = pl.pallas_call(
+        window_kernel,
+        out_shape=jax.ShapeDtypeStruct((16, LEVELS, 128), F32),
+        in_specs=[whole, whole],
+        out_specs=whole,
+        scratch_shapes=[
+            pltpu.VMEM((16, 136, 128), F32),
+            pltpu.VMEM((4, 576, 128), F32),
+            pltpu.VMEM((8, LEVELS, 256), F32),
+            pltpu.VMEM((8, LEVELS, 256), F32),
+            pltpu.VMEM((8, LEVELS, 3 * LEVELS), BF16),
+            pltpu.VMEM((8, 2, LEVELS, 256), F32),
+            pltpu.VMEM((STEPS, LEVELS, 256), F32),
+            pltpu.VMEM((2, 2, 288, 128), F32),
+            pltpu.VMEM((2, 2 * LEVELS, 512), BF16),
+            pltpu.VMEM((2, 512, 128), jnp.int32),
+            dma((15,)), dma((16,)), dma((15,)), dma((16,)),
+            dma((STEPS,)), dma((STEPS,)), dma((16,)), dma((16,)),
+        ],
+        compiler_params=pltpu.CompilerParams(
+            collective_id=0, has_side_effects=True, vmem_limit_bytes=40 << 20
+        ),
+    )(pm, wind_rows)
+    return out.reshape(16, 18, 4, 128).transpose(2, 1, 0, 3)
+
+
 def solution(mesh):
+    sizes = dict(mesh.shape)
+    small = (sizes["lat"], sizes["lon"], sizes["lev"]) == (4, 2, 4)
     return jax.shard_map(
-        shards,
+        fast_shards if small else shards,
         mesh=mesh,
         in_specs=(
             P("lat", "lev", None, "lon"),

time: 262 us -> 57.3 us (0.22)
  the two profiles are of different devices: /device:TPU:0 before, /device:TPU:29 now
where the time goes in v1:
time: 57.3 us; the launch traced here: 57 us
  Pallas kernels  51.4 us (90%)
  local copies, waits for them, and re-layouts  4.69 us (8%)
  between operations  0.73 us (1%)
    pallas_call x1, Pallas kernels, fast_shards(): pl.pallas_call(window_kernel, out_shape=jax.ShapeDtypeStruct((16, LEVELS,...  51.4 us
    unnamed x14, local copies, waits for them, and re-layouts  3.64 us

profile of v1, /device:TPU:29, one launch (start us, length us, event | category | flops | bytes accessed | tf_op | source)
XLA Modules:
  0.0 57.0 jit_solution(10867506371231623952)
XLA Ops:
  0.7 0.0 copy-start.4
  0.7 0.0 copy-start.5
  0.7 0.6 %copy-done.4 = s32[64]{0:T(128)S(1)} copy-done((s32[64]{0:T(128)S(1)}, s32[64]{0:T(128)}, u32[]{:S(2)}) %copy-start.4) | copy-done | bytes 280
  1.3 0.0 copy-done.5
  1.4 0.0 copy-start.3
  1.4 0.1 copy.15
  1.5 0.6 %copy-done.3 = f32[64,16]{0,1:T(8,128)S(1)} copy-done((f32[64,16]{0,1:T(8,128)S(1)}, f32[64,16]{0,1:T(8,128)}, u32[]{:S(2)}) %copy-start.3) | copy-done | bytes 4120
  2.1 0.1 copy.13
  2.1 0.0 copy-start.1
  2.1 0.1 broadcast_multiply_fusion
  2.2 0.7 %copy-done.1 = f32[1,72,72]{2,1,0:T(8,128)S(1)} copy-done((f32[1,72,72]{2,1,0:T(8,128)S(1)}, f32[1,72,72]{2,1,0:T(8,128)}, u32[]{:S(2)}) %copy-start.1) | copy-done | bytes 20760
  2.9 0.1 copy.16
  3.0 0.0 copy-start.2
  3.0 0.7 %copy-done.2 = f32[64,72]{1,0:T(8,128)S(1)} copy-done((f32[64,72]{1,0:T(8,128)S(1)}, f32[64,72]{1,0:T(8,128)}, u32[]{:S(2)}) %copy-start.2) | copy-done | bytes 18456
  3.8 0.0 copy-start
  3.8 0.1 select_maximum_fusion.pm_ref
  3.8 0.8 %copy-done = f32[4,18,2,128]{3,2,1,0:T(2,128)S(1)} copy-done((f32[4,18,2,128]{3,2,1,0:T(2,128)S(1)}, f32[4,18,2,128]{3,2,1,0:T(2,128)}, u32[]{:S(2)}) %copy-start) | copy-done | bytes 73752
  4.7 51.4 %shard_map.73 = f32[16,72,128]{2,1,0:T(8,128)S(1)} custom-call(f32[136,128]{1,0:T(8,128)S(1)} %select_maximum_fusion.pm_ref, f32[144,128]{1,0:T(8,128)S(1)} %bitcast.29), custom_call_target="tpu_custom_call" | custom-call | tf_op jit(solution)/shard_map/pallas_call | solution.py:346
  56.1 0.9 %copy.20 = f32[16,18,4,128]{3,0,1,2:T(8,128)} copy(f32[16,18,4,128]{3,2,1,0:T(4,128)S(1)} %bitcast.28) | data formatting | bytes 1179648 | tf_op jit(solution)/shard_map/reshape | solution.py:369
  (4 shorter events, 0.0 us)
Async XLA Ops:
  0.7 0.7 %copy-start.4 = (s32[64]{0:T(128)S(1)}, s32[64]{0:T(128)}, u32[]{:S(2)}) copy-start(s32[64]{0:T(128)} %param.11) | copy-start | bytes 772
  0.7 0.7 %copy-start.5 = (s32[64,1]{0,1:T(1,128)S(1)}, s32[64,1]{0,1:T(1,128)}, u32[]{:S(2)}) copy-start(s32[64,1]{0,1:T(1,128)} %param.12) | copy-start | bytes 772
  1.4 0.7 %copy-start.3 = (f32[64,16]{0,1:T(8,128)S(1)}, f32[64,16]{0,1:T(8,128)}, u32[]{:S(2)}) copy-start(f32[64,16]{0,1:T(8,128)} %param.10) | copy-start | bytes 12292
  2.1 0.8 %copy-start.1 = (f32[1,72,72]{2,1,0:T(8,128)S(1)}, f32[1,72,72]{2,1,0:T(8,128)}, u32[]{:S(2)}) copy-start(f32[1,72,72]{2,1,0:T(8,128)} %param.8) | copy-start | bytes 62212
  3.0 0.8 %copy-start.2 = (f32[64,72]{1,0:T(8,128)S(1)}, f32[64,72]{1,0:T(8,128)}, u32[]{:S(2)}) copy-start(f32[64,72]{1,0:T(8,128)} %param.9) | copy-start | bytes 55300
  3.8 0.9 %copy-start = (f32[4,18,2,128]{3,2,1,0:T(2,128)S(1)}, f32[4,18,2,128]{3,2,1,0:T(2,128)}, u32[]{:S(2)}) copy-start(f32[4,18,2,128]{3,2,1,0:T(2,128)} %param.7) | copy-start | bytes 221188

commit v2 on v0

--- a/solution.py
+++ b/solution.py
@@ -1,6 +1,8 @@
 import jax
 import jax.numpy as jnp
 from jax import lax
+from jax.experimental import pallas as pl
+from jax.experimental.pallas import tpu as pltpu
 from jax.sharding import PartitionSpec as P
 
 STEPS = 4
@@ -81,9 +83,313 @@
     return gradient
 
 
+LEVELS = 72
+TRACERS = 16
+PACK = 92
+MESH = pl.DeviceIdType.MESH
+F32 = jnp.float32
+BF16 = jnp.bfloat16
+
+
+def window_kernel(
+    pm_ref, w_ref, out_ref, gp, gw, mixed, mix_stack, wind, halo, stage, vals, spots,
+    send_p, recv_p, send_w, recv_w, send_h, recv_h, send_o, recv_o,
+):
+    lat, o, z = lax.axis_index("lat"), lax.axis_index("lon"), lax.axis_index("lev")
+    y, x = lat // 2, lat % 2
+    me = (x * 2 + o) * 4 + z
+    other_x, other_o = (lat - x) + (1 - x), 1 - o
+    across = (1 - y) * 2 + x
+
+    def member(s):
+        return ((lat - x) + s // 8, (s // 4) % 2, s % 4)
+
+    def device_of(d):
+        return member((me + d) % 16)
+
+    barrier = pltpu.get_barrier_semaphore()
+    for d in range(1, 16):
+        pl.semaphore_signal(barrier, inc=1, device_id=device_of(d), device_id_type=MESH)
+    pl.semaphore_signal(barrier, inc=1, device_id=(across, o, z), device_id_type=MESH)
+    pl.semaphore_wait(barrier, 16)
+
+    def make(refs, at, src, send, recv, xx, oo, zz, k, device):
+        return pltpu.make_async_remote_copy(
+            src_ref=at(xx, oo, zz) if src is None else src,
+            dst_ref=at(xx, oo, zz),
+            send_sem=send.at[k],
+            recv_sem=recv.at[(xx * 2 + oo) * 4 + zz],
+            device_id=device,
+            device_id_type=MESH,
+        )
+
+    def at_p(xx, oo, zz):
+        return gp.at[(xx * 2 + oo) * 4 + zz]
+
+    def at_w(xx, oo, zz):
+        return gw.at[xx * 2 + oo, pl.ds(pl.multiple_of(zz * 144, 8), 144)]
+
+    sent = []
+
+    def line(d):
+        q = jnp.minimum(z, 3 - z)
+        f = d - q if d == 1 else d
+        return z if d == 0 else f + (z // 2) * (3 - 2 * f)
+
+    def launch(copy):
+        copy.start()
+        sent.append(copy)
+
+    def first(at, src, send, recv):
+        for d in range(1, 4):
+            launch(make(None, at, src, send, recv, x, o, z, d - 1, (lat, o, line(d))))
+        launch(make(None, at, src, send, recv, x, o, z, 3, (other_x, o, z)))
+        launch(make(None, at, src, send, recv, x, o, z, 7, (lat, other_o, z)))
+
+    def second(at, send, recv, d):
+        zz = line(d)
+        make(None, at, None, send, recv, x, o, zz, 0, (lat, o, z)).wait_recv()
+        launch(make(None, at, None, send, recv, x, o, zz, 3 + d, (other_x, o, z)))
+        launch(make(None, at, None, send, recv, x, o, zz, 7 + d, (lat, other_o, z)))
+
+    def third(at, send, recv, d):
+        zz = line(d)
+        make(None, at, None, send, recv, 1 - x, o, zz, 0, (lat, o, z)).wait_recv()
+        launch(make(None, at, None, send, recv, 1 - x, o, zz, 11 + d, (lat, other_o, z)))
+
+    def rest(at, send, recv):
+        for xx in (x, 1 - x):
+            for d in range(4):
+                make(None, at, None, send, recv, xx, 1 - o, line(d), 0, (lat, o, z)).wait_recv()
+
+    first(at_p, pm_ref, send_p, recv_p)
+    first(at_w, w_ref, send_w, recv_w)
+    gp[me] = pm_ref[...]
+    gw[x * 2 + o, pl.ds(pl.multiple_of(z * 144, 8), 144)] = w_ref[...]
+    third(at_p, send_p, recv_p, 0)
+    for d in range(1, 4):
+        second(at_p, send_p, recv_p, d)
+    for d in range(1, 4):
+        third(at_p, send_p, recv_p, d)
+    third(at_w, send_w, recv_w, 0)
+    second(at_w, send_w, recv_w, 1)
+    rest(at_p, send_p, recv_p)
+
+    def place(n):
+        return y * n + (1 - y) * (7 - n)
+
+    lane = lax.broadcasted_iota(jnp.int32, (512, 128), 1)
+    wide = lax.broadcasted_iota(jnp.int32, (512, 256), 1)
+    for xx in range(2):
+        rows = gp[xx * 8:xx * 8 + 8, 0:64, :].reshape(512, 128)
+        resid = jnp.sum(jnp.where(lane == LEVELS + me, rows, 0.0), axis=1, keepdims=True)
+        spot = jnp.sum(jnp.where(lane == LEVELS + TRACERS, rows, 0.0), axis=1, keepdims=True)
+        spots[xx] = jnp.broadcast_to(spot, (512, 128)).astype(jnp.int32)
+        terms = (rows * resid).T[:LEVELS]
+        high = terms.astype(BF16).astype(F32)
+        vals[xx] = jnp.concatenate([high, terms - high], axis=0).astype(BF16)
+
+    def mix(n, col):
+        high = col.astype(BF16).astype(F32)
+        stack = jnp.concatenate([high, high, col - high], axis=0).astype(BF16)
+        return jnp.dot(mix_stack[n], stack, preferred_element_type=F32)
+
+    def begin(n):
+        i = place(n)
+        left = gp[(i // 4) * 8 + i % 4, :, PACK:]
+        right = gp[(i // 4) * 8 + 4 + i % 4, :, PACK:]
+        mat = jnp.concatenate([left, right], axis=1)
+        high = mat.astype(BF16).astype(F32)
+        mix_stack[n] = jnp.concatenate([high, mat - high, high], axis=1).astype(BF16)
+        spot = spots[i // 4]
+        hits = jnp.concatenate([spot, spot], axis=1) == wide + (i % 4) * 256
+        ones = jnp.where(hits, 1.0, 0.0).astype(BF16)
+        both = jnp.dot(vals[i // 4], ones, preferred_element_type=F32)
+        mixed[0, n] = mix(n, both[:LEVELS] + both[LEVELS:])
+
+    def winds_in(n):
+        i = place(n)
+        for half in range(2):
+            for comp in range(2):
+                part = gw[(i // 4) * 2 + half, pl.ds((i % 4) * 2 + comp, LEVELS, stride=8), :]
+                if comp == 1:
+                    part = part * (1 - 2 * y).astype(F32)
+                wind[n, comp, :, half * 128:half * 128 + 128] = part
+
+    def halo_copy(step):
+        return pltpu.make_async_remote_copy(
+            src_ref=mixed.at[step, 0],
+            dst_ref=halo.at[step],
+            send_sem=send_h.at[step],
+            recv_sem=recv_h.at[step],
+            device_id=(across, o, z),
+            device_id_type=MESH,
+        )
+
+    def moved(step, n):
+        c = mixed[step, n]
+        if n == 0:
+            halo_copy(step).wait_recv()
+            before = halo[step]
+        else:
+            before = mixed[step, n - 1]
+        after = mixed[step, min(n + 1, 7)]
+        u, v = wind[n, 0], wind[n, 1]
+        east = pltpu.roll(c, 255, axis=1)
+        west = pltpu.roll(c, 1, axis=1)
+        return (
+            c
+            + jnp.maximum(u, 0.0) * (east - c)
+            + jnp.minimum(u, 0.0) * (c - west)
+            + jnp.maximum(v, 0.0) * (before - c)
+            + jnp.minimum(v, 0.0) * (c - after)
+        )
+
+    def advance(step, n):
+        new = moved(step - 1, n)
+        mixed[step, n] = mix(n, new)
+        if n == 0:
+            launch(halo_copy(step))
+
+    def finish(n):
+        new = moved(STEPS - 1, n)
+        i = place(n)
+        for half in range(2):
+            stage[i // 4, half, pl.ds(i % 4, LEVELS, stride=4), :] = new[:, half * 128:half * 128 + 128]
+
+    out_sends = []
+
+    def ship(far):
+        xx = y if far else 1 - y
+        for d in (3, 2, 1, 0):
+            for turn in range(2):
+                half = (o + turn) % 2 if d == 0 else turn
+                zz = line(d)
+                k = (0 if far else 8) + turn * 4 + d
+                source = stage.at[xx, half, pl.ds(pl.multiple_of(zz * 72, 8), 72)]
+                copy = pltpu.make_async_remote_copy(
+                    src_ref=source,
+                    dst_ref=out_ref.at[me],
+                    send_sem=send_o.at[k],
+                    recv_sem=recv_o.at[me],
+                    device_id=((lat - x) + xx, half, zz),
+                    device_id_type=MESH,
+                )
+                if d or turn:
+                    copy.start()
+                    out_sends.append((None, copy))
+                else:
+                    mine = xx == x
+
+                    @pl.when(mine)
+                    def _():
+                        out_ref[me] = source[...]
+
+                    @pl.when(jnp.logical_not(mine))
+                    def _():
+                        copy.start()
+
+                    out_sends.append((mine, copy))
+
+    begin(0)
+    launch(halo_copy(0))
+    second(at_w, send_w, recv_w, 2)
+    begin(1)
+    begin(2)
+    second(at_w, send_w, recv_w, 3)
+    third(at_w, send_w, recv_w, 1)
+    begin(3)
+    begin(4)
+    third(at_w, send_w, recv_w, 2)
+    begin(5)
+    begin(6)
+    begin(7)
+    third(at_w, send_w, recv_w, 3)
+    rest(at_w, send_w, recv_w)
+    for n in range(8):
+        winds_in(n)
+    for n in range(8):
+        advance(1, n)
+    for n in (7, 6, 5, 4, 3, 2, 0, 1):
+        advance(2, n)
+    for n in (7, 6, 5, 4, 3):
+        advance(3, n)
+    for n in (7, 6, 5, 4):
+        finish(n)
+    ship(True)
+    for n in (0, 1, 2):
+        advance(3, n)
+    for n in (3, 2, 1, 0):
+        finish(n)
+    ship(False)
+    for mine, copy in out_sends:
+        if mine is None:
+            copy.wait_send()
+        else:
+
+            @pl.when(jnp.logical_not(mine))
+            def _():
+                copy.wait_send()
+
+    for d in range(1, 16):
+        s = (me + d) % 16
+        pltpu.make_async_remote_copy(
+            src_ref=out_ref.at[s],
+            dst_ref=out_ref.at[s],
+            send_sem=send_o.at[0],
+            recv_sem=recv_o.at[s],
+            device_id=(lat, o, z),
+            device_id_type=MESH,
+        ).wait_recv()
+    for one in sent:
+        one.wait_send()
+
+
+def fast_shards(winds, mixing, kernels, residuals, columns, owners, live_counts):
+    row_count = kernels.shape[0]
+    live = (jnp.arange(row_count) < live_counts[0]).astype(F32)
+    own = owners[:, 0]
+    spot = (own % 4) * 256 + (own // 4) * 128 + columns % 128
+    rows = jnp.concatenate(
+        [kernels, residuals * live[:, None], spot.astype(F32)[:, None],
+         jnp.zeros((row_count, PACK - LEVELS - TRACERS - 1), F32)], axis=1)
+    rows = jnp.pad(rows, ((0, LEVELS - row_count), (0, 0)))
+    matrix = mixing[0].T
+    matrix = jnp.where(lax.axis_index("lon") == 0, matrix[:, :LEVELS // 2], matrix[:, LEVELS // 2:])
+    pm = jnp.concatenate([rows, matrix], axis=1)
+    wind_rows = winds.transpose(1, 0, 2, 3).reshape(144, 128)
+    dma = pltpu.SemaphoreType.DMA
+    whole = pl.BlockSpec(memory_space=pltpu.VMEM)
+    out = pl.pallas_call(
+        window_kernel,
+        out_shape=jax.ShapeDtypeStruct((16, LEVELS, 128), F32),
+        in_specs=[whole, whole],
+        out_specs=whole,
+        scratch_shapes=[
+            pltpu.VMEM((16, LEVELS, 128), F32),
+            pltpu.VMEM((4, 576, 128), F32),
+            pltpu.VMEM((STEPS, 8, LEVELS, 256), F32),
+            pltpu.VMEM((8, LEVELS, 3 * LEVELS), BF16),
+            pltpu.VMEM((8, 2, LEVELS, 256), F32),
+            pltpu.VMEM((STEPS, LEVELS, 256), F32),
+            pltpu.VMEM((2, 2, 288, 128), F32),
+            pltpu.VMEM((2, 2 * LEVELS, 512), BF16),
+            pltpu.VMEM((2, 512, 128), jnp.int32),
+            dma((15,)), dma((16,)), dma((15,)), dma((16,)),
+            dma((STEPS,)), dma((STEPS,)), dma((16,)), dma((16,)),
+        ],
+        compiler_params=pltpu.CompilerParams(
+            collective_id=0, has_side_effects=True, vmem_limit_bytes=40 << 20
+        ),
+    )(pm, wind_rows)
+    return out.reshape(16, 18, 4, 128).transpose(2, 1, 0, 3)
+
+
 def solution(mesh):
+    sizes = dict(mesh.shape)
+    small = (sizes["lat"], sizes["lon"], sizes["lev"]) == (4, 2, 4)
     return jax.shard_map(
-        shards,
+        fast_shards if small else shards,
         mesh=mesh,
         in_specs=(
             P("lat", "lev", None, "lon"),

time: 262 us -> 46.9 us (0.18)
  the two profiles are of different devices: /device:TPU:0 before, /device:TPU:11 now
where the time goes in v2:
time: 46.9 us; the launch traced here: 46.5 us
  Pallas kernels  40.8 us (87%)
  local copies, waits for them, and re-layouts  4.71 us (10%)
  between operations  0.72 us (2%)
    pallas_call x1, Pallas kernels, fast_shards(): pl.pallas_call(window_kernel, out_shape=jax.ShapeDtypeStruct((16, LEVELS,...  40.8 us
    unnamed x14, local copies, waits for them, and re-layouts  3.59 us

profile of v2, /device:TPU:11, one launch (start us, length us, event | category | flops | bytes accessed | tf_op | source)
XLA Modules:
  0.0 46.5 jit_solution(1479032223422532981)
XLA Ops:
  0.7 0.0 copy-start.4
  0.7 0.0 copy-start.5
  0.7 0.6 %copy-done.4 = s32[64]{0:T(128)S(1)} copy-done((s32[64]{0:T(128)S(1)}, s32[64]{0:T(128)}, u32[]{:S(2)}) %copy-start.4) | copy-done | bytes 280
  1.3 0.0 copy-done.5
  1.4 0.1 pad.10.clone
  1.4 0.0 copy-start.3
  1.4 0.1 copy.15
  1.5 0.6 %copy-done.3 = f32[64,16]{0,1:T(8,128)S(1)} copy-done((f32[64,16]{0,1:T(8,128)S(1)}, f32[64,16]{0,1:T(8,128)}, u32[]{:S(2)}) %copy-start.3) | copy-done | bytes 4120
  2.1 0.1 copy.13
  2.2 0.0 copy-start.2
  2.2 0.1 broadcast_multiply_fusion
  2.3 0.7 %copy-done.2 = f32[64,72]{1,0:T(8,128)S(1)} copy-done((f32[64,72]{1,0:T(8,128)S(1)}, f32[64,72]{1,0:T(8,128)}, u32[]{:S(2)}) %copy-start.2) | copy-done | bytes 18456
  3.0 0.0 copy-start.1
  3.0 0.1 maximum_maximum_fusion
  3.1 0.7 %copy-done.1 = f32[1,72,72]{2,1,0:T(8,128)S(1)} copy-done((f32[1,72,72]{2,1,0:T(8,128)S(1)}, f32[1,72,72]{2,1,0:T(8,128)}, u32[]{:S(2)}) %copy-start.1) | copy-done | bytes 20760
  3.7 0.1 copy.16
  3.8 0.1 slice_select_fusion
  3.9 0.0 copy-start
  3.9 0.1 select_maximum_fusion.pm_ref
  4.0 0.8 %copy-done = f32[4,18,2,128]{3,2,1,0:T(2,128)S(1)} copy-done((f32[4,18,2,128]{3,2,1,0:T(2,128)S(1)}, f32[4,18,2,128]{3,2,1,0:T(2,128)}, u32[]{:S(2)}) %copy-start) | copy-done | bytes 73752
  4.8 40.8 %shard_map.73 = f32[16,72,128]{2,1,0:T(8,128)S(1)} custom-call(f32[72,128]{1,0:T(8,128)S(1)} %select_maximum_fusion.pm_ref, f32[144,128]{1,0:T(8,128)S(1)} %bitcast.29), custom_call_target="tpu_custom_call" | custom-call | tf_op jit(solution)/shard_map/pallas_call | solution.py:363
  45.6 0.9 %copy.20 = f32[16,18,4,128]{3,0,1,2:T(8,128)} copy(f32[16,18,4,128]{3,2,1,0:T(4,128)S(1)} %bitcast.28) | data formatting | bytes 1179648 | tf_op jit(solution)/shard_map/reshape | solution.py:385
  (4 shorter events, 0.0 us)
Async XLA Ops:
  0.7 0.7 %copy-start.4 = (s32[64]{0:T(128)S(1)}, s32[64]{0:T(128)}, u32[]{:S(2)}) copy-start(s32[64]{0:T(128)} %param.11) | copy-start | bytes 772
  0.7 0.7 %copy-start.5 = (s32[64,1]{0,1:T(1,128)S(1)}, s32[64,1]{0,1:T(1,128)}, u32[]{:S(2)}) copy-start(s32[64,1]{0,1:T(1,128)} %param.12) | copy-start | bytes 772
  1.4 0.7 %copy-start.3 = (f32[64,16]{0,1:T(8,128)S(1)}, f32[64,16]{0,1:T(8,128)}, u32[]{:S(2)}) copy-start(f32[64,16]{0,1:T(8,128)} %param.10) | copy-start | bytes 12292
  2.2 0.8 %copy-start.2 = (f32[64,72]{1,0:T(8,128)S(1)}, f32[64,72]{1,0:T(8,128)}, u32[]{:S(2)}) copy-start(f32[64,72]{1,0:T(8,128)} %param.9) | copy-start | bytes 55300
  3.0 0.8 %copy-start.1 = (f32[1,72,72]{2,1,0:T(8,128)S(1)}, f32[1,72,72]{2,1,0:T(8,128)}, u32[]{:S(2)}) copy-start(f32[1,72,72]{2,1,0:T(8,128)} %param.8) | copy-start | bytes 62212
  3.9 0.9 %copy-start = (f32[4,18,2,128]{3,2,1,0:T(2,128)S(1)}, f32[4,18,2,128]{3,2,1,0:T(2,128)}, u32[]{:S(2)}) copy-start(f32[4,18,2,128]{3,2,1,0:T(2,128)} %param.7) | copy-start | bytes 221188

commit v3 on v2

--- a/solution.py
+++ b/solution.py
@@ -92,8 +92,8 @@
 
 
 def window_kernel(
-    pm_ref, w_ref, out_ref, gp, gw, mixed, mix_stack, wind, halo, stage, vals, spots,
-    send_p, recv_p, send_w, recv_w, send_h, recv_h, send_o, recv_o,
+    pm_ref, w_ref, out_ref, gp, gw, mixed, mix_stack, wind, stage, vals, spots,
+    send_p, recv_p, send_w, recv_w, send_o, recv_o,
 ):
     lat, o, z = lax.axis_index("lat"), lax.axis_index("lon"), lax.axis_index("lev")
     y, x = lat // 2, lat % 2
@@ -157,8 +157,26 @@
         make(None, at, None, send, recv, 1 - x, o, zz, 0, (lat, o, z)).wait_recv()
         launch(make(None, at, None, send, recv, 1 - x, o, zz, 11 + d, (lat, other_o, z)))
 
-    def rest(at, send, recv):
-        for xx in (x, 1 - x):
+        launch(across_copy(at, send, recv, d))
+
+    def across_copy(at, send, recv, d):
+        zz = line(d)
+        return pltpu.make_async_remote_copy(
+            src_ref=at(1 - y, o, zz),
+            dst_ref=at(2, o, zz),
+            send_sem=send.at[15 + d],
+            recv_sem=recv.at[16 + o * 4 + zz],
+            device_id=(across, o, z),
+            device_id_type=MESH,
+        )
+
+    def fifth(at, send, recv, d):
+        zz = line(d)
+        make(None, at, None, send, recv, 2, o, zz, 0, (lat, o, z)).wait_recv()
+        launch(make(None, at, None, send, recv, 2, o, zz, 19 + d, (lat, other_o, z)))
+
+    def rest(at, send, recv, groups):
+        for xx in groups:
             for d in range(4):
                 make(None, at, None, send, recv, xx, 1 - o, line(d), 0, (lat, o, z)).wait_recv()
 
@@ -173,26 +191,30 @@
         third(at_p, send_p, recv_p, d)
     third(at_w, send_w, recv_w, 0)
     second(at_w, send_w, recv_w, 1)
-    rest(at_p, send_p, recv_p)
+    rest(at_p, send_p, recv_p, (x, 1 - x))
+    base = (x * 2 + o) * 4 + (z % 2) * 2
+    partner = z + 1 - 2 * (z % 2)
 
     def place(n):
-        return y * n + (1 - y) * (7 - n)
+        return y * (n if n >= 0 else n + 12) + (1 - y) * (7 - n)
 
     lane = lax.broadcasted_iota(jnp.int32, (512, 128), 1)
     wide = lax.broadcasted_iota(jnp.int32, (512, 256), 1)
-    for xx in range(2):
+    def spread(xx):
         rows = gp[xx * 8:xx * 8 + 8, 0:64, :].reshape(512, 128)
-        resid = jnp.sum(jnp.where(lane == LEVELS + me, rows, 0.0), axis=1, keepdims=True)
         spot = jnp.sum(jnp.where(lane == LEVELS + TRACERS, rows, 0.0), axis=1, keepdims=True)
         spots[xx] = jnp.broadcast_to(spot, (512, 128)).astype(jnp.int32)
-        terms = (rows * resid).T[:LEVELS]
-        high = terms.astype(BF16).astype(F32)
-        vals[xx] = jnp.concatenate([high, terms - high], axis=0).astype(BF16)
+        for t in range(2):
+            resid = jnp.sum(jnp.where(lane == LEVELS + base + t, rows, 0.0), axis=1, keepdims=True)
+            terms = (rows * resid).T[:LEVELS]
+            high = terms.astype(BF16).astype(F32)
+            both = jnp.concatenate([high, terms - high], axis=0).astype(BF16)
+            vals[xx, t * 2 * LEVELS:(t + 1) * 2 * LEVELS] = both
 
     def mix(n, col):
         high = col.astype(BF16).astype(F32)
         stack = jnp.concatenate([high, high, col - high], axis=0).astype(BF16)
-        return jnp.dot(mix_stack[n], stack, preferred_element_type=F32)
+        return jnp.dot(mix_stack[n + 4], stack, preferred_element_type=F32)
 
     def begin(n):
         i = place(n)
@@ -200,12 +222,14 @@
         right = gp[(i // 4) * 8 + 4 + i % 4, :, PACK:]
         mat = jnp.concatenate([left, right], axis=1)
         high = mat.astype(BF16).astype(F32)
-        mix_stack[n] = jnp.concatenate([high, mat - high, high], axis=1).astype(BF16)
+        mix_stack[n + 4] = jnp.concatenate([high, mat - high, high], axis=1).astype(BF16)
         spot = spots[i // 4]
         hits = jnp.concatenate([spot, spot], axis=1) == wide + (i % 4) * 256
         ones = jnp.where(hits, 1.0, 0.0).astype(BF16)
         both = jnp.dot(vals[i // 4], ones, preferred_element_type=F32)
-        mixed[0, n] = mix(n, both[:LEVELS] + both[LEVELS:])
+        for t in range(2):
+            part = both[t * 2 * LEVELS:(t + 1) * 2 * LEVELS]
+            mixed[t, 0, n + 4] = mix(n, part[:LEVELS] + part[LEVELS:])
 
     def winds_in(n):
         i = place(n)
@@ -214,27 +238,13 @@
                 part = gw[(i // 4) * 2 + half, pl.ds((i % 4) * 2 + comp, LEVELS, stride=8), :]
                 if comp == 1:
                     part = part * (1 - 2 * y).astype(F32)
-                wind[n, comp, :, half * 128:half * 128 + 128] = part
-
-    def halo_copy(step):
-        return pltpu.make_async_remote_copy(
-            src_ref=mixed.at[step, 0],
-            dst_ref=halo.at[step],
-            send_sem=send_h.at[step],
-            recv_sem=recv_h.at[step],
-            device_id=(across, o, z),
-            device_id_type=MESH,
-        )
-
-    def moved(step, n):
-        c = mixed[step, n]
-        if n == 0:
-            halo_copy(step).wait_recv()
-            before = halo[step]
-        else:
-            before = mixed[step, n - 1]
-        after = mixed[step, min(n + 1, 7)]
-        u, v = wind[n, 0], wind[n, 1]
+                wind[n + 4, comp, :, half * 128:half * 128 + 128] = part
+
+    def moved(t, step, n):
+        c = mixed[t, step, n + 4]
+        before = mixed[t, step, n + 3]
+        after = mixed[t, step, min(n + 1, 7) + 4]
+        u, v = wind[n + 4, 0], wind[n + 4, 1]
         east = pltpu.roll(c, 255, axis=1)
         west = pltpu.roll(c, 1, axis=1)
         return (
@@ -245,37 +255,33 @@
             + jnp.minimum(v, 0.0) * (c - after)
         )
 
-    def advance(step, n):
-        new = moved(step - 1, n)
-        mixed[step, n] = mix(n, new)
-        if n == 0:
-            launch(halo_copy(step))
-
-    def finish(n):
-        new = moved(STEPS - 1, n)
+    def advance(t, step, n):
+        mixed[t, step, n + 4] = mix(n, moved(t, step - 1, n))
+
+    def finish(t, n):
+        new = moved(t, STEPS - 1, n)
         i = place(n)
         for half in range(2):
-            stage[i // 4, half, pl.ds(i % 4, LEVELS, stride=4), :] = new[:, half * 128:half * 128 + 128]
+            stage[t, i // 4, half, pl.ds(i % 4, LEVELS, stride=4), :] = new[:, half * 128:half * 128 + 128]
 
     out_sends = []
 
-    def ship(far):
+    def ship(t, far):
         xx = y if far else 1 - y
-        for d in (3, 2, 1, 0):
+        for away in (1, 0):
             for turn in range(2):
-                half = (o + turn) % 2 if d == 0 else turn
-                zz = line(d)
-                k = (0 if far else 8) + turn * 4 + d
-                source = stage.at[xx, half, pl.ds(pl.multiple_of(zz * 72, 8), 72)]
+                half = (o + turn) % 2
+                zz = partner if away else z
+                source = stage.at[t, xx, half, pl.ds(pl.multiple_of(zz * 72, 8), 72)]
                 copy = pltpu.make_async_remote_copy(
                     src_ref=source,
-                    dst_ref=out_ref.at[me],
-                    send_sem=send_o.at[k],
-                    recv_sem=recv_o.at[me],
+                    dst_ref=out_ref.at[base + t],
+                    send_sem=send_o.at[t * 8 + (0 if far else 4) + turn * 2 + away],
+                    recv_sem=recv_o.at[base + t],
                     device_id=((lat - x) + xx, half, zz),
                     device_id_type=MESH,
                 )
-                if d or turn:
+                if away or turn:
                     copy.start()
                     out_sends.append((None, copy))
                 else:
@@ -283,7 +289,7 @@
 
                     @pl.when(mine)
                     def _():
-                        out_ref[me] = source[...]
+                        out_ref[base + t] = source[...]
 
                     @pl.when(jnp.logical_not(mine))
                     def _():
@@ -291,37 +297,57 @@
 
                     out_sends.append((mine, copy))
 
-    begin(0)
-    launch(halo_copy(0))
+    def far_side(t):
+        for step in range(1, STEPS):
+            for n in range(7, step - 1, -1):
+                advance(t, step, n)
+        for n in (7, 6, 5, 4):
+            finish(t, n)
+        ship(t, True)
+
+    def near_side(t):
+        for step in range(1, STEPS):
+            for n in range(step - 1, step - 5, -1):
+                advance(t, step, n)
+        for n in (3, 2, 1, 0):
+            finish(t, n)
+        ship(t, False)
+
+    spread(0)
+    spread(1)
+    begin(7)
     second(at_w, send_w, recv_w, 2)
-    begin(1)
-    begin(2)
+    begin(6)
+    begin(5)
     second(at_w, send_w, recv_w, 3)
     third(at_w, send_w, recv_w, 1)
+    begin(4)
+    for d in range(4):
+        fifth(at_p, send_p, recv_p, d)
     begin(3)
-    begin(4)
     third(at_w, send_w, recv_w, 2)
-    begin(5)
-    begin(6)
-    begin(7)
+    begin(2)
+    begin(1)
+    begin(0)
     third(at_w, send_w, recv_w, 3)
-    rest(at_w, send_w, recv_w)
+    rest(at_w, send_w, recv_w, (x, 1 - x))
+    fifth(at_w, send_w, recv_w, 0)
     for n in range(8):
         winds_in(n)
-    for n in range(8):
-        advance(1, n)
-    for n in (7, 6, 5, 4, 3, 2, 0, 1):
-        advance(2, n)
-    for n in (7, 6, 5, 4, 3):
-        advance(3, n)
-    for n in (7, 6, 5, 4):
-        finish(n)
-    ship(True)
-    for n in (0, 1, 2):
-        advance(3, n)
-    for n in (3, 2, 1, 0):
-        finish(n)
-    ship(False)
+    fifth(at_w, send_w, recv_w, 1)
+    far_side(0)
+    fifth(at_w, send_w, recv_w, 2)
+    fifth(at_w, send_w, recv_w, 3)
+    far_side(1)
+    rest(at_p, send_p, recv_p, (2,))
+    spread(2)
+    for n in (-1, -2, -3, -4):
+        begin(n)
+    rest(at_w, send_w, recv_w, (2,))
+    for n in (-1, -2, -3):
+        winds_in(n)
+    near_side(0)
+    near_side(1)
     for mine, copy in out_sends:
         if mine is None:
             copy.wait_send()
@@ -331,8 +357,8 @@
             def _():
                 copy.wait_send()
 
-    for d in range(1, 16):
-        s = (me + d) % 16
+    for d in range(2, 16):
+        s = (base + d) % 16
         pltpu.make_async_remote_copy(
             src_ref=out_ref.at[s],
             dst_ref=out_ref.at[s],
@@ -366,17 +392,16 @@
         in_specs=[whole, whole],
         out_specs=whole,
         scratch_shapes=[
-            pltpu.VMEM((16, LEVELS, 128), F32),
-            pltpu.VMEM((4, 576, 128), F32),
-            pltpu.VMEM((STEPS, 8, LEVELS, 256), F32),
-            pltpu.VMEM((8, LEVELS, 3 * LEVELS), BF16),
-            pltpu.VMEM((8, 2, LEVELS, 256), F32),
-            pltpu.VMEM((STEPS, LEVELS, 256), F32),
-            pltpu.VMEM((2, 2, 288, 128), F32),
-            pltpu.VMEM((2, 2 * LEVELS, 512), BF16),
-            pltpu.VMEM((2, 512, 128), jnp.int32),
-            dma((15,)), dma((16,)), dma((15,)), dma((16,)),
-            dma((STEPS,)), dma((STEPS,)), dma((16,)), dma((16,)),
+            pltpu.VMEM((24, LEVELS, 128), F32),
+            pltpu.VMEM((6, 576, 128), F32),
+            pltpu.VMEM((2, STEPS, 12, LEVELS, 256), F32),
+            pltpu.VMEM((12, LEVELS, 3 * LEVELS), BF16),
+            pltpu.VMEM((12, 2, LEVELS, 256), F32),
+            pltpu.VMEM((2, 2, 2, 288, 128), F32),
+            pltpu.VMEM((3, 4 * LEVELS, 512), BF16),
+            pltpu.VMEM((3, 512, 128), jnp.int32),
+            dma((23,)), dma((24,)), dma((23,)), dma((24,)),
+            dma((16,)), dma((16,)),
         ],
         compiler_params=pltpu.CompilerParams(
             collective_id=0, has_side_effects=True, vmem_limit_bytes=40 << 20

time: 46.9 us -> 43.2 us (0.921)
  the two profiles are of different devices: /device:TPU:11 before, /device:TPU:0 now
where the time goes in v3:
time: 43.2 us; the launch traced here: 42.9 us
  Pallas kernels  37.1 us (86%)
  local copies, waits for them, and re-layouts  4.71 us (11%)
  between operations  0.72 us (2%)
    pallas_call x1, Pallas kernels, fast_shards(): pl.pallas_call(window_kernel, out_shape=jax.ShapeDtypeStruct((16, LEVELS,...  37.1 us
    unnamed x14, local copies, waits for them, and re-layouts  3.59 us
    reshape x1, local copies, waits for them, and re-layouts, fast_shards(): return out.reshape(16, 18, 4, 128).transpose(2, 1, 0, 3)  0.92 us

profile of v3, /device:TPU:0, one launch (start us, length us, event | category | flops | bytes accessed | tf_op | source)
XLA Modules:
  0.0 42.9 jit_solution(10596126787690295606)
XLA Ops:
  0.7 0.0 copy-start.4
  0.7 0.0 copy-start.5
  0.7 0.6 %copy-done.4 = s32[64]{0:T(128)S(1)} copy-done((s32[64]{0:T(128)S(1)}, s32[64]{0:T(128)}, u32[]{:S(2)}) %copy-start.4) | copy-done | bytes 280
  1.3 0.0 copy-done.5
  1.4 0.1 pad.10.clone
  1.4 0.0 copy-start.3
  1.4 0.1 copy.15
  1.5 0.6 %copy-done.3 = f32[64,16]{0,1:T(8,128)S(1)} copy-done((f32[64,16]{0,1:T(8,128)S(1)}, f32[64,16]{0,1:T(8,128)}, u32[]{:S(2)}) %copy-start.3) | copy-done | bytes 4120
  2.1 0.1 copy.13
  2.2 0.0 copy-start.2
  2.2 0.1 broadcast_multiply_fusion
  2.3 0.7 %copy-done.2 = f32[64,72]{1,0:T(8,128)S(1)} copy-done((f32[64,72]{1,0:T(8,128)S(1)}, f32[64,72]{1,0:T(8,128)}, u32[]{:S(2)}) %copy-start.2) | copy-done | bytes 18456
  3.0 0.0 copy-start.1
  3.0 0.1 maximum_maximum_fusion
  3.1 0.7 %copy-done.1 = f32[1,72,72]{2,1,0:T(8,128)S(1)} copy-done((f32[1,72,72]{2,1,0:T(8,128)S(1)}, f32[1,72,72]{2,1,0:T(8,128)}, u32[]{:S(2)}) %copy-start.1) | copy-done | bytes 20760
  3.7 0.1 copy.16
  3.8 0.1 slice_select_fusion
  3.9 0.0 copy-start
  3.9 0.1 select_maximum_fusion.pm_ref
  4.0 0.8 %copy-done = f32[4,18,2,128]{3,2,1,0:T(2,128)S(1)} copy-done((f32[4,18,2,128]{3,2,1,0:T(2,128)S(1)}, f32[4,18,2,128]{3,2,1,0:T(2,128)}, u32[]{:S(2)}) %copy-start) | copy-done | bytes 73752
  4.8 37.1 %shard_map.73 = f32[16,72,128]{2,1,0:T(8,128)S(1)} custom-call(f32[72,128]{1,0:T(8,128)S(1)} %select_maximum_fusion.pm_ref, f32[144,128]{1,0:T(8,128)S(1)} %bitcast.29), custom_call_target="tpu_custom_call" | custom-call | tf_op jit(solution)/shard_map/pallas_call | solution.py:389
  41.9 0.9 %copy.20 = f32[16,18,4,128]{3,0,1,2:T(8,128)} copy(f32[16,18,4,128]{3,2,1,0:T(4,128)S(1)} %bitcast.28) | data formatting | bytes 1179648 | tf_op jit(solution)/shard_map/reshape | solution.py:410
  (4 shorter events, 0.0 us)
Async XLA Ops:
  0.7 0.7 %copy-start.4 = (s32[64]{0:T(128)S(1)}, s32[64]{0:T(128)}, u32[]{:S(2)}) copy-start(s32[64]{0:T(128)} %param.11) | copy-start | bytes 772
  0.7 0.7 %copy-start.5 = (s32[64,1]{0,1:T(1,128)S(1)}, s32[64,1]{0,1:T(1,128)}, u32[]{:S(2)}) copy-start(s32[64,1]{0,1:T(1,128)} %param.12) | copy-start | bytes 772
  1.4 0.7 %copy-start.3 = (f32[64,16]{0,1:T(8,128)S(1)}, f32[64,16]{0,1:T(8,128)}, u32[]{:S(2)}) copy-start(f32[64,16]{0,1:T(8,128)} %param.10) | copy-start | bytes 12292
  2.2 0.8 %copy-start.2 = (f32[64,72]{1,0:T(8,128)S(1)}, f32[64,72]{1,0:T(8,128)}, u32[]{:S(2)}) copy-start(f32[64,72]{1,0:T(8,128)} %param.9) | copy-start | bytes 55300
  3.0 0.8 %copy-start.1 = (f32[1,72,72]{2,1,0:T(8,128)S(1)}, f32[1,72,72]{2,1,0:T(8,128)}, u32[]{:S(2)}) copy-start(f32[1,72,72]{2,1,0:T(8,128)} %param.8) | copy-start | bytes 62212
  3.9 0.9 %copy-start = (f32[4,18,2,128]{3,2,1,0:T(2,128)S(1)}, f32[4,18,2,128]{3,2,1,0:T(2,128)}, u32[]{:S(2)}) copy-start(f32[4,18,2,128]{3,2,1,0:T(2,128)} %param.7) | copy-start | bytes 221188

commit v4 on v3

--- a/solution.py
+++ b/solution.py
@@ -92,8 +92,9 @@
 
 
 def window_kernel(
-    pm_ref, w_ref, out_ref, gp, gw, mixed, mix_stack, wind, stage, vals, spots,
-    send_p, recv_p, send_w, recv_w, send_o, recv_o,
+    mat_ref, kern_ref, res_ref, col_ref, own_ref, live_ref, w_ref, out_ref,
+    mat_in, kern_in, res_in, col_in, own_in, gp, gw, mixed, mix_stack, wind, stage, vals, spots,
+    load, send_p, recv_p, send_w, recv_w, send_o, recv_o,
 ):
     lat, o, z = lax.axis_index("lat"), lax.axis_index("lon"), lax.axis_index("lev")
     y, x = lat // 2, lat % 2
@@ -111,6 +112,30 @@
     for d in range(1, 16):
         pl.semaphore_signal(barrier, inc=1, device_id=device_of(d), device_id_type=MESH)
     pl.semaphore_signal(barrier, inc=1, device_id=(across, o, z), device_id_type=MESH)
+    loads = [
+        pltpu.make_async_copy(source, into, load.at[k])
+        for k, (source, into) in enumerate(
+            [(kern_ref, kern_in), (mat_ref, mat_in), (res_ref, res_in), (col_ref, col_in), (own_ref, own_in)]
+        )
+    ]
+    for one in loads:
+        one.start()
+    gw[x * 2 + o, pl.ds(pl.multiple_of(z * 144, 8), 144)] = w_ref[...]
+    for one in loads:
+        one.wait()
+    slots = kern_in.shape[0]
+    alive = lax.broadcasted_iota(jnp.int32, (TRACERS, slots), 1) < live_ref[0]
+    own = own_in[...]
+    half_of = (own >= 4).astype(jnp.int32)
+    spot_row = ((own - 4 * half_of) * 256 + half_of * 128 + col_in[...]).astype(F32)
+    side = jnp.concatenate(
+        [jnp.where(alive, res_in[...], 0.0), jnp.broadcast_to(spot_row, (8, slots))], axis=0
+    ).T
+    top = jnp.concatenate([kern_in[...], side[:, :PACK - LEVELS]], axis=1)
+    top = jnp.concatenate([top, jnp.zeros((LEVELS - slots, PACK), F32)], axis=0)
+    turned = mat_in[...].T
+    turned = jnp.where(o == 0, turned[:, :LEVELS // 2], turned[:, LEVELS // 2:])
+    gp[me] = jnp.concatenate([top, turned], axis=1)
     pl.semaphore_wait(barrier, 16)
 
     def make(refs, at, src, send, recv, xx, oo, zz, k, device):
@@ -180,10 +205,8 @@
             for d in range(4):
                 make(None, at, None, send, recv, xx, 1 - o, line(d), 0, (lat, o, z)).wait_recv()
 
-    first(at_p, pm_ref, send_p, recv_p)
+    first(at_p, None, send_p, recv_p)
     first(at_w, w_ref, send_w, recv_w)
-    gp[me] = pm_ref[...]
-    gw[x * 2 + o, pl.ds(pl.multiple_of(z * 144, 8), 144)] = w_ref[...]
     third(at_p, send_p, recv_p, 0)
     for d in range(1, 4):
         second(at_p, send_p, recv_p, d)
@@ -373,25 +396,21 @@
 
 def fast_shards(winds, mixing, kernels, residuals, columns, owners, live_counts):
     row_count = kernels.shape[0]
-    live = (jnp.arange(row_count) < live_counts[0]).astype(F32)
-    own = owners[:, 0]
-    spot = (own % 4) * 256 + (own // 4) * 128 + columns % 128
-    rows = jnp.concatenate(
-        [kernels, residuals * live[:, None], spot.astype(F32)[:, None],
-         jnp.zeros((row_count, PACK - LEVELS - TRACERS - 1), F32)], axis=1)
-    rows = jnp.pad(rows, ((0, LEVELS - row_count), (0, 0)))
-    matrix = mixing[0].T
-    matrix = jnp.where(lax.axis_index("lon") == 0, matrix[:, :LEVELS // 2], matrix[:, LEVELS // 2:])
-    pm = jnp.concatenate([rows, matrix], axis=1)
     wind_rows = winds.transpose(1, 0, 2, 3).reshape(144, 128)
     dma = pltpu.SemaphoreType.DMA
+    far = pl.BlockSpec(memory_space=pltpu.HBM)
     whole = pl.BlockSpec(memory_space=pltpu.VMEM)
     out = pl.pallas_call(
         window_kernel,
         out_shape=jax.ShapeDtypeStruct((16, LEVELS, 128), F32),
-        in_specs=[whole, whole],
+        in_specs=[far] * 5 + [pl.BlockSpec(memory_space=pltpu.SMEM), whole],
         out_specs=whole,
         scratch_shapes=[
+            pltpu.VMEM((LEVELS, LEVELS), F32),
+            pltpu.VMEM((row_count, LEVELS), F32),
+            pltpu.VMEM((TRACERS, row_count), F32),
+            pltpu.VMEM((1, row_count), jnp.int32),
+            pltpu.VMEM((1, row_count), jnp.int32),
             pltpu.VMEM((24, LEVELS, 128), F32),
             pltpu.VMEM((6, 576, 128), F32),
             pltpu.VMEM((2, STEPS, 12, LEVELS, 256), F32),
@@ -400,13 +419,16 @@
             pltpu.VMEM((2, 2, 2, 288, 128), F32),
             pltpu.VMEM((3, 4 * LEVELS, 512), BF16),
             pltpu.VMEM((3, 512, 128), jnp.int32),
-            dma((23,)), dma((24,)), dma((23,)), dma((24,)),
+            dma((5,)), dma((23,)), dma((24,)), dma((23,)), dma((24,)),
             dma((16,)), dma((16,)),
         ],
         compiler_params=pltpu.CompilerParams(
             collective_id=0, has_side_effects=True, vmem_limit_bytes=40 << 20
         ),
-    )(pm, wind_rows)
+    )(
+        mixing[0], kernels, residuals.T, columns.reshape(1, row_count),
+        owners.reshape(1, row_count), live_counts, wind_rows,
+    )
     return out.reshape(16, 18, 4, 128).transpose(2, 1, 0, 3)
 
 

time: 43.2 us -> 40.4 us (0.935)
  local copies, waits for them, and re-layouts: 4.71 us -> 2.49 us
    unnamed x14 -> x10, local copies, waits for them, and re-layouts: 3.59 us -> 0.64 us
    transpose x1, local copies, waits for them, and re-layouts: 0.03 us -> 0.93 us  [fast_shards(): wind_rows = winds.transpose(1, 0, 2, 3).reshape(144, 128)]
where the time goes in v4:
time: 40.4 us; the launch traced here: 40.3 us
  Pallas kernels  37.1 us (92%)
  local copies, waits for them, and re-layouts  2.49 us (6%)
  between operations  0.73 us (2%)
    pallas_call x1, Pallas kernels, fast_shards(): pl.pallas_call(window_kernel, out_shape=jax.ShapeDtypeStruct((16, LEVELS,...  37.1 us
    transpose x1, local copies, waits for them, and re-layouts, fast_shards(): wind_rows = winds.transpose(1, 0, 2, 3).reshape(144, 128)  0.93 us
    reshape x1, local copies, waits for them, and re-layouts, fast_shards(): return out.reshape(16, 18, 4, 128).transpose(2, 1, 0, 3)  0.92 us

profile of v4, /device:TPU:0, one launch (start us, length us, event | category | flops | bytes accessed | tf_op | source)
XLA Modules:
  0.0 40.3 jit_solution(2160373900186373755)
XLA Ops:
  0.7 0.0 copy-start
  0.7 0.0 copy-start.1
  0.7 0.0 copy-start.2
  0.7 0.9 %copy.8 = f32[18,4,2,128]{3,2,1,0:T(2,128)S(1)} copy(f32[18,4,2,128]{3,2,0,1:T(2,128)} %bitcast.16) | data formatting | bytes 147456 | tf_op jit(solution)/shard_map/transpose | solution.py:399
  1.6 0.0 copy-start.3
  1.6 0.0 copy-start.4
  1.6 0.0 copy-done
  1.6 0.0 copy-done.1
  1.7 0.0 copy-done.2
  1.7 0.6 %copy-done.3 = s32[64]{0:T(128)S(1)} copy-done((s32[64]{0:T(128)S(1)}, s32[64]{0:T(128)}, u32[]{:S(2)}) %copy-start.3) | copy-done | bytes 280
  2.3 0.0 copy-done.4
  2.3 37.1 %shard_map.73 = f32[16,72,128]{2,1,0:T(8,128)S(1)} custom-call(f32[72,72]{1,0:T(8,128)S(1)} %bitcast.12, f32[64,72]{1,0:T(8,128)S(1)} %copy-done.1, f32[16,64]{1,0:T(8,128)S(1)} %bitcast.13, s32[1,64]{1,0:T(1,128)S(1)} %bitcast.14, s32[1,64]{1,0:T(1,128)S(1)} %bitcast.15, s32[1]{0:T(128)S(6)} %copy.12.live_ref, f32[144,128]{1,0:T(8,128)S(1)} %bitcast.11), custom_call_target="tpu_custom_call" | custom-call | tf_op jit(solution)/shard_map/pallas_call | solution.py:403
  39.4 0.9 %copy.11 = f32[16,18,4,128]{3,0,1,2:T(8,128)} copy(f32[16,18,4,128]{3,2,1,0:T(4,128)S(1)} %bitcast.10) | data formatting | bytes 1179648 | tf_op jit(solution)/shard_map/reshape | solution.py:432
Async XLA Ops:
  0.7 1.0 %copy-start = (f32[1,72,72]{2,1,0:T(8,128)S(1)}, f32[1,72,72]{2,1,0:T(8,128)}, u32[]{:S(2)}) copy-start(f32[1,72,72]{2,1,0:T(8,128)} %param.8) | copy-start | bytes 62212
  0.7 1.0 %copy-start.1 = (f32[64,72]{1,0:T(8,128)S(1)}, f32[64,72]{1,0:T(8,128)}, u32[]{:S(2)}) copy-start(f32[64,72]{1,0:T(8,128)} %kern_ref.1) | copy-start | bytes 55300
  0.7 1.0 %copy-start.2 = (f32[64,16]{0,1:T(8,128)S(1)}, f32[64,16]{0,1:T(8,128)}, u32[]{:S(2)}) copy-start(f32[64,16]{0,1:T(8,128)} %param.10) | copy-start | bytes 12292
  1.6 0.7 %copy-start.3 = (s32[64]{0:T(128)S(1)}, s32[64]{0:T(128)}, u32[]{:S(2)}) copy-start(s32[64]{0:T(128)} %param.11) | copy-start | bytes 772
  1.6 0.7 %copy-start.4 = (s32[64,1]{0,1:T(1,128)S(1)}, s32[64,1]{0,1:T(1,128)}, u32[]{:S(2)}) copy-start(s32[64,1]{0,1:T(1,128)} %param.12) | copy-start | bytes 772
